TPU v7x, 256 devices: a whole 4x4x8 slice. The times are simulated.
256 devices in a mesh: section: 8 (over y, core), chan: 32 (over z, x).
Axes of the slice: x: 4, y: 4, z: 8, core: 2. Of those that a mesh axis runs over, the one named last changes fastest.
Arguments:
- prompt: bfloat16 [192, 8192], P(None, 'chan'), may hold values from -6 to 6
- norm_gain: bfloat16 [8, 8192], P('section', 'chan'), may hold values from 0.5 to 1.5
- in_weight: bfloat16 [8, 8192, 3, 8192], P('section', None, None, 'chan'), may hold values from -0.0625 to 0.0625
- feat_taps: float32 [8, 3, 3, 8192], P('section', None, None, 'chan'), may hold values from -3 to 3
- fir_taps: float32 [8, 128, 512], P('section', None, 'chan'), may hold values from -0.5 to 0.5
- residues: float32 [8, 16, 512], P('section', None, 'chan'), may hold values from -0.2 to 0.2
- decay: float32 [8, 16, 512], P('section', None, 'chan'), may hold values from 0.002 to 0.1
Outputs:
- section_out: bfloat16 [8, 192, 8192], P('section', None, 'chan')
All inputs are finite; a program needn't handle non-finite values.
Results may differ from a plain program's by a relative error of at most 0.019.
Values may be sent and summed in bfloat16 or wider, within the bound.
A program may use at most 128 MiB of HBM per device.

v0:
```python
import jax
import jax.numpy as jnp
from jax import lax
from jax.sharding import PartitionSpec as P

BLOCK_TOK = 64
NBLOCKS = 3
EPSILON = 1e-06


def shifted(value, axis, steps):
    count = lax.axis_size(axis)
    initial, last = (max(0, -steps), min(count, count - steps))
    return lax.ppermute(value, axis, [(source, source + steps) for source in range(initial, last)])


def body(prompt, norm_gain, in_weight, feat_taps, fir_taps, residues, decay):
    block_len = BLOCK_TOK
    num_blocks = NBLOCKS
    width = in_weight.shape[1]
    local = prompt.shape[1]
    groups_local = fir_taps.shape[2]
    group_size = local // groups_local
    fir_len = fir_taps.shape[1]
    sections = lax.axis_size("section")
    section_idx = lax.axis_index("section")
    is_medium = section_idx % 2 == 0
    weight = in_weight[0].reshape(width, 3 * local)
    tap_rows = feat_taps[0]
    fir_section = fir_taps[0]
    residue_section = residues[0]
    rate_section = decay[0]
    out_pos = jnp.arange(block_len)
    in_pos = jnp.arange(fir_len + block_len)
    fir_lag = out_pos[:, None] + fir_len - in_pos[None, :]
    fir_ok = (fir_lag >= 0) & (fir_lag < fir_len)
    fir_table = jnp.where(fir_ok[None], fir_section.T[:, jnp.clip(fir_lag, 0, fir_len - 1)], 0.0)
    inner_lag = out_pos[:, None] - (in_pos[None, :] - fir_len)
    inner_ok = (inner_lag >= 0) & (in_pos[None, :] >= fir_len)
    lag_values = out_pos.astype(jnp.float32)
    powers = jnp.exp(-rate_section[None, :, :] * lag_values[:, None, None])
    modal = jnp.einsum("ng,jng->jg", residue_section, powers, precision=lax.Precision.HIGHEST)
    modal_table = jnp.where(inner_ok[None], modal.T[:, jnp.clip(inner_lag, 0, block_len - 1)], 0.0)
    toeplitz = jnp.where(is_medium, fir_table, modal_table)
    carry_coef = residue_section[None] * jnp.exp(
        -rate_section[None] * (lag_values + 1.0)[:, None, None]
    )
    carry_coef = jnp.where(is_medium, 0.0, carry_coef)
    feed_coef = jnp.exp(-rate_section[None] * (block_len - 1.0 - lag_values)[:, None, None])
    block_decay = jnp.exp(-rate_section * block_len)

    def add_rows(shard_piece):
        return jnp.dot(shard_piece, weight, preferred_element_type=jnp.float32)

    def turn(carried, turn_index):
        incoming, proj_cache, kv_cache, modal_state, out_buffer = carried
        which = turn_index - section_idx
        is_live = (which >= 0) & (which < num_blocks)
        begin_row = jnp.clip(which, 0, num_blocks - 1) * block_len
        first_rows = lax.dynamic_slice_in_dim(prompt, begin_row, block_len, 0)
        rows_in = jnp.where(section_idx == 0, first_rows, incoming)
        inputs_f = rows_in.astype(jnp.float32)
        partial_sq = jnp.sum(inputs_f * inputs_f, axis=1)
        squares = lax.psum(partial_sq, "chan")
        normed = (
            inputs_f * lax.rsqrt(squares[:, None] / width + EPSILON) * norm_gain.astype(jnp.float32)
        ).astype(jnp.bfloat16)
        projected = add_rows(lax.all_gather(normed, "chan", axis=1, tiled=True))
        projected = projected.reshape(block_len, 3, local)
        extended = jnp.concatenate([proj_cache, projected], axis=0)
        features = (
            tap_rows[0] * extended[2:] + tap_rows[1] * extended[1:-1] + tap_rows[2] * extended[:-2]
        )
        product_kv = features[:, 1] * features[:, 2]
        window = jnp.concatenate([kv_cache, product_kv], axis=0)
        grouped = window.reshape(fir_len + block_len, groups_local, group_size)
        convolved = jnp.einsum("gts,sgk->tgk", toeplitz, grouped, precision=lax.Precision.HIGHEST)
        convolved = convolved + jnp.einsum(
            "tng,ngk->tgk", carry_coef, modal_state, precision=lax.Precision.HIGHEST
        )
        new_state = block_decay[:, :, None] * modal_state + jnp.einsum(
            "tng,tgk->ngk", feed_coef, grouped[fir_len:], precision=lax.Precision.HIGHEST
        )
        result = (inputs_f + features[:, 0] * convolved.reshape(block_len, local)).astype(
            jnp.bfloat16
        )
        proj_cache = jnp.where(is_live, extended[block_len:], proj_cache)
        kv_cache = jnp.where(is_live, window[block_len:], kv_cache)
        modal_state = jnp.where(is_live, new_state, modal_state)
        out_buffer = jnp.where(
            is_live, lax.dynamic_update_slice_in_dim(out_buffer, result, begin_row, 0), out_buffer
        )
        passed = shifted(result, "section", 1)
        return ((passed, proj_cache, kv_cache, modal_state, out_buffer), None)

    initial = (
        jnp.zeros((block_len, local), jnp.bfloat16),
        jnp.zeros((2, 3, local), jnp.float32),
        jnp.zeros((fir_len, local), jnp.float32),
        jnp.zeros((residues.shape[1], groups_local, group_size), jnp.float32),
        jnp.zeros((block_len * num_blocks, local), jnp.bfloat16),
    )
    finals, unused = lax.scan(turn, initial, jnp.arange(num_blocks + sections - 1, dtype=jnp.int32))
    return finals[4][None]


def solution(mesh):
    return jax.shard_map(
        body,
        mesh=mesh,
        in_specs=(
            P(None, "chan"),
            P("section", "chan"),
            P("section", None, None, "chan"),
            P("section", None, None, "chan"),
            P("section", None, "chan"),
            P("section", None, "chan"),
            P("section", None, "chan"),
        ),
        out_specs=P("section", None, "chan"),
        check_vma=False,
    )
```

profile of v0, /device:TPU:1, one launch (start us, length us, event | category | flops | bytes accessed | tf_op | source)
XLA Modules:
  0.0 1730.6 jit_solution(16256413265977966794)
XLA Ops:
  7.2 16.7 copy.26
  41.1 41.1 %gather_fusion.1 = f32[12288,16]{1,0:T(8,128)} fusion(f32[16,64]{0,1:T(8,128)S(1)} %multiply_reduce_fusion, s32[12288]{0:T(1024)S(1)} %broadcast_clamp_fusion), kind=kCustom, calls=%fused_computation.1 | custom fusion | bytes 1622016 | tf_op jit(solution)/shard_map/gather | solution.py:43
  87.5 41.1 %gather_fusion = f32[12288,16]{1,0:T(8,128)} fusion(f32[16,128]{0,1:T(8,128)S(1)} %bitcast.82, s32[12288]{0:T(1024)S(1)} %broadcast_clamp_fusion.1), kind=kCustom, calls=%fused_computation | custom fusion | bytes 1622016 | tf_op jit(solution)/shard_map/gather | solution.py:37
  133.9 1589.2 %while.22 = (s32[]{:T(128)}, bf16[64,256]{1,0:T(8,128)(2,1)S(1)}, f32[2,3,256]{2,1,0:T(4,128)S(1)}, f32[128,256]{0,1:T(8,128)S(1)}, f32[16,16,16]{0,2,1:T(8,128)...) while((s32[]{:T(128)}, bf16[64,256]{1,0:T(8,128)(2,1)S(1)}, ...), condition=%wide.region_3.4_spmd.clone.clone.clone, body=%wide.region_0.3_spmd.clone.clone.clone.sunk | while | flops 850173312 | bytes 21374916 | solution.py:103
  136.1 64.3 %psum.12 = f32[64]{0:T(128)S(1)} all-reduce(f32[64]{0:T(128)S(1)} %get-tuple-element.554), channel_id=1, replica_groups=mesh['section'=8,'chan'=32] {'chan'}, use_global_device_ids=true, to_apply=%region_2.2 | all-reduce | flops 64 | bytes 512 | tf_op jit(solution)/shard_map/while/body/eval_jaxpr/psum | solution.py:64
  201.2 76.1 %all-gather.2.cloned.1.call-done = bf16[64,8192]{1,0:T(8,128)(2,1)} async-done(((bf16[64,256]{1,0:T(8,128)(2,1)}), bf16[64,8192]{1,0:T(8,128)(2,1)}) %all-gather.2.cloned.1.call-update) | async-done | bytes 1048592 | tf_op jit(solution)/shard_map/while/body/eval_jaxpr/all_gather | solution.py:68
  297.3 59.9 %psum.12 = f32[64]{0:T(128)S(1)} all-reduce(f32[64]{0:T(128)S(1)} %get-tuple-element.554), channel_id=1, replica_groups=mesh['section'=8,'chan'=32] {'chan'}, use_global_device_ids=true, to_apply=%region_2.2 | all-reduce | flops 64 | bytes 512 | tf_op jit(solution)/shard_map/while/body/eval_jaxpr/psum | solution.py:64
  357.9 78.0 %all-gather.2.cloned.1.call-done = bf16[64,8192]{1,0:T(8,128)(2,1)} async-done(((bf16[64,256]{1,0:T(8,128)(2,1)}), bf16[64,8192]{1,0:T(8,128)(2,1)}) %all-gather.2.cloned.1.call-update) | async-done | bytes 1048592 | tf_op jit(solution)/shard_map/while/body/eval_jaxpr/all_gather | solution.py:68
  455.9 59.9 %psum.12 = f32[64]{0:T(128)S(1)} all-reduce(f32[64]{0:T(128)S(1)} %get-tuple-element.554), channel_id=1, replica_groups=mesh['section'=8,'chan'=32] {'chan'}, use_global_device_ids=true, to_apply=%region_2.2 | all-reduce | flops 64 | bytes 512 | tf_op jit(solution)/shard_map/while/body/eval_jaxpr/psum | solution.py:64
  516.6 78.0 %all-gather.2.cloned.1.call-done = bf16[64,8192]{1,0:T(8,128)(2,1)} async-done(((bf16[64,256]{1,0:T(8,128)(2,1)}), bf16[64,8192]{1,0:T(8,128)(2,1)}) %all-gather.2.cloned.1.call-update) | async-done | bytes 1048592 | tf_op jit(solution)/shard_map/while/body/eval_jaxpr/all_gather | solution.py:68
  614.6 59.9 %psum.12 = f32[64]{0:T(128)S(1)} all-reduce(f32[64]{0:T(128)S(1)} %get-tuple-element.554), channel_id=1, replica_groups=mesh['section'=8,'chan'=32] {'chan'}, use_global_device_ids=true, to_apply=%region_2.2 | all-reduce | flops 64 | bytes 512 | tf_op jit(solution)/shard_map/while/body/eval_jaxpr/psum | solution.py:64
  675.2 78.0 %all-gather.2.cloned.1.call-done = bf16[64,8192]{1,0:T(8,128)(2,1)} async-done(((bf16[64,256]{1,0:T(8,128)(2,1)}), bf16[64,8192]{1,0:T(8,128)(2,1)}) %all-gather.2.cloned.1.call-update) | async-done | bytes 1048592 | tf_op jit(solution)/shard_map/while/body/eval_jaxpr/all_gather | solution.py:68
  773.3 59.9 %psum.12 = f32[64]{0:T(128)S(1)} all-reduce(f32[64]{0:T(128)S(1)} %get-tuple-element.554), channel_id=1, replica_groups=mesh['section'=8,'chan'=32] {'chan'}, use_global_device_ids=true, to_apply=%region_2.2 | all-reduce | flops 64 | bytes 512 | tf_op jit(solution)/shard_map/while/body/eval_jaxpr/psum | solution.py:64
  833.9 78.0 %all-gather.2.cloned.1.call-done = bf16[64,8192]{1,0:T(8,128)(2,1)} async-done(((bf16[64,256]{1,0:T(8,128)(2,1)}), bf16[64,8192]{1,0:T(8,128)(2,1)}) %all-gather.2.cloned.1.call-update) | async-done | bytes 1048592 | tf_op jit(solution)/shard_map/while/body/eval_jaxpr/all_gather | solution.py:68
  931.9 59.9 %psum.12 = f32[64]{0:T(128)S(1)} all-reduce(f32[64]{0:T(128)S(1)} %get-tuple-element.554), channel_id=1, replica_groups=mesh['section'=8,'chan'=32] {'chan'}, use_global_device_ids=true, to_apply=%region_2.2 | all-reduce | flops 64 | bytes 512 | tf_op jit(solution)/shard_map/while/body/eval_jaxpr/psum | solution.py:64
  992.6 78.0 %all-gather.2.cloned.1.call-done = bf16[64,8192]{1,0:T(8,128)(2,1)} async-done(((bf16[64,256]{1,0:T(8,128)(2,1)}), bf16[64,8192]{1,0:T(8,128)(2,1)}) %all-gather.2.cloned.1.call-update) | async-done | bytes 1048592 | tf_op jit(solution)/shard_map/while/body/eval_jaxpr/all_gather | solution.py:68
  1090.6 59.9 %psum.12 = f32[64]{0:T(128)S(1)} all-reduce(f32[64]{0:T(128)S(1)} %get-tuple-element.554), channel_id=1, replica_groups=mesh['section'=8,'chan'=32] {'chan'}, use_global_device_ids=true, to_apply=%region_2.2 | all-reduce | flops 64 | bytes 512 | tf_op jit(solution)/shard_map/while/body/eval_jaxpr/psum | solution.py:64
  1151.2 78.0 %all-gather.2.cloned.1.call-done = bf16[64,8192]{1,0:T(8,128)(2,1)} async-done(((bf16[64,256]{1,0:T(8,128)(2,1)}), bf16[64,8192]{1,0:T(8,128)(2,1)}) %all-gather.2.cloned.1.call-update) | async-done | bytes 1048592 | tf_op jit(solution)/shard_map/while/body/eval_jaxpr/all_gather | solution.py:68
  1249.3 59.9 %psum.12 = f32[64]{0:T(128)S(1)} all-reduce(f32[64]{0:T(128)S(1)} %get-tuple-element.554), channel_id=1, replica_groups=mesh['section'=8,'chan'=32] {'chan'}, use_global_device_ids=true, to_apply=%region_2.2 | all-reduce | flops 64 | bytes 512 | tf_op jit(solution)/shard_map/while/body/eval_jaxpr/psum | solution.py:64
  1309.9 78.0 %all-gather.2.cloned.1.call-done = bf16[64,8192]{1,0:T(8,128)(2,1)} async-done(((bf16[64,256]{1,0:T(8,128)(2,1)}), bf16[64,8192]{1,0:T(8,128)(2,1)}) %all-gather.2.cloned.1.call-update) | async-done | bytes 1048592 | tf_op jit(solution)/shard_map/while/body/eval_jaxpr/all_gather | solution.py:68
  1407.9 59.9 %psum.12 = f32[64]{0:T(128)S(1)} all-reduce(f32[64]{0:T(128)S(1)} %get-tuple-element.554), channel_id=1, replica_groups=mesh['section'=8,'chan'=32] {'chan'}, use_global_device_ids=true, to_apply=%region_2.2 | all-reduce | flops 64 | bytes 512 | tf_op jit(solution)/shard_map/while/body/eval_jaxpr/psum | solution.py:64
  1468.6 78.0 %all-gather.2.cloned.1.call-done = bf16[64,8192]{1,0:T(8,128)(2,1)} async-done(((bf16[64,256]{1,0:T(8,128)(2,1)}), bf16[64,8192]{1,0:T(8,128)(2,1)}) %all-gather.2.cloned.1.call-update) | async-done | bytes 1048592 | tf_op jit(solution)/shard_map/while/body/eval_jaxpr/all_gather | solution.py:68
  1566.6 59.9 %psum.12 = f32[64]{0:T(128)S(1)} all-reduce(f32[64]{0:T(128)S(1)} %get-tuple-element.554), channel_id=1, replica_groups=mesh['section'=8,'chan'=32] {'chan'}, use_global_device_ids=true, to_apply=%region_2.2 | all-reduce | flops 64 | bytes 512 | tf_op jit(solution)/shard_map/while/body/eval_jaxpr/psum | solution.py:64
  1627.2 78.0 %all-gather.2.cloned.1.call-done = bf16[64,8192]{1,0:T(8,128)(2,1)} async-done(((bf16[64,256]{1,0:T(8,128)(2,1)}), bf16[64,8192]{1,0:T(8,128)(2,1)}) %all-gather.2.cloned.1.call-update) | async-done | bytes 1048592 | tf_op jit(solution)/shard_map/while/body/eval_jaxpr/all_gather | solution.py:68
  (299 shorter events, 228.8 us)
Async XLA Ops:
  23.9 16.7 copy-start.4
  23.9 16.8 copy-start.1
  40.6 46.6 %copy-start.3 = (f32[1,128,16]{1,2,0:T(8,128)S(1)}, f32[1,128,16]{1,2,0:T(8,128)}, u32[]{:S(2)}) copy-start(f32[1,128,16]{1,2,0:T(8,128)} %param.13) | copy-start | bytes 24580
  82.3 51.6 %copy-start.2 = (bf16[1,256]{1,0:T(2,128)(2,1)S(1)}, bf16[1,256]{1,0:T(2,128)(2,1)}, u32[]{:S(2)}) copy-start(bf16[1,256]{1,0:T(2,128)(2,1)} %param.10) | copy-start | bytes 1540
  133.9 143.3 %all-gather.2.cloned.1.call-start = ((), (), s32[]{:S(2)}) async-start(), calls=%async_computation | async-start | bytes 1081344 | tf_op jit(solution)/shard_map/while/body/eval_jaxpr/all_gather | solution.py:68
  286.4 8.7 collective-permute-start
  295.1 140.8 %all-gather.2.cloned.1.call-start = ((), (), s32[]{:S(2)}) async-start(), calls=%async_computation | async-start | bytes 1081344 | tf_op jit(solution)/shard_map/while/body/eval_jaxpr/all_gather | solution.py:68
  445.0 8.7 collective-permute-start
  453.8 140.8 %all-gather.2.cloned.1.call-start = ((), (), s32[]{:S(2)}) async-start(), calls=%async_computation | async-start | bytes 1081344 | tf_op jit(solution)/shard_map/while/body/eval_jaxpr/all_gather | solution.py:68
  603.7 8.7 collective-permute-start
  612.5 140.8 %all-gather.2.cloned.1.call-start = ((), (), s32[]{:S(2)}) async-start(), calls=%async_computation | async-start | bytes 1081344 | tf_op jit(solution)/shard_map/while/body/eval_jaxpr/all_gather | solution.py:68
  762.4 8.7 collective-permute-start
  771.1 140.8 %all-gather.2.cloned.1.call-start = ((), (), s32[]{:S(2)}) async-start(), calls=%async_computation | async-start | bytes 1081344 | tf_op jit(solution)/shard_map/while/body/eval_jaxpr/all_gather | solution.py:68
  921.0 8.7 collective-permute-start
  929.8 140.8 %all-gather.2.cloned.1.call-start = ((), (), s32[]{:S(2)}) async-start(), calls=%async_computation | async-start | bytes 1081344 | tf_op jit(solution)/shard_map/while/body/eval_jaxpr/all_gather | solution.py:68
  1079.7 8.7 collective-permute-start
  1088.5 140.8 %all-gather.2.cloned.1.call-start = ((), (), s32[]{:S(2)}) async-start(), calls=%async_computation | async-start | bytes 1081344 | tf_op jit(solution)/shard_map/while/body/eval_jaxpr/all_gather | solution.py:68
  1238.4 8.7 collective-permute-start
  1247.1 140.8 %all-gather.2.cloned.1.call-start = ((), (), s32[]{:S(2)}) async-start(), calls=%async_computation | async-start | bytes 1081344 | tf_op jit(solution)/shard_map/while/body/eval_jaxpr/all_gather | solution.py:68
  1397.0 8.7 collective-permute-start
  1405.8 140.8 %all-gather.2.cloned.1.call-start = ((), (), s32[]{:S(2)}) async-start(), calls=%async_computation | async-start | bytes 1081344 | tf_op jit(solution)/shard_map/while/body/eval_jaxpr/all_gather | solution.py:68
  1555.7 8.7 collective-permute-start
  1564.4 140.8 %all-gather.2.cloned.1.call-start = ((), (), s32[]{:S(2)}) async-start(), calls=%async_computation | async-start | bytes 1081344 | tf_op jit(solution)/shard_map/while/body/eval_jaxpr/all_gather | solution.py:68
  1714.4 8.7 collective-permute-start
  (1 other events, 0.6 us)
Sparse Core Ops, SparseCore 0:
  201.3 75.9 all-gather.1
  358.0 77.8 all-gather.1
  516.6 77.8 all-gather.1
  675.3 77.8 all-gather.1
  834.0 77.8 all-gather.1
  992.6 77.8 all-gather.1
  1151.3 77.8 all-gather.1
  1310.0 77.8 all-gather.1
  1468.6 77.8 all-gather.1
  1627.3 77.8 all-gather.1
where the time goes:
time: 1730 us
  waiting for transfers between devices  783 us (45%)
  blocking collectives  603 us (35%)
  local copies, waits for them, and re-layouts  136 us (8%)
  matrix products  88.7 us (5%)
  starting transfers between devices  77.4 us (4%)
  other arithmetic  20.9 us (1%)
    all_gather x10, waiting for transfers between devices, turn(): projected = add_rows(lax.all_gather(normed, 'chan', axis=1, tiled=True))  778 us
    psum x10, blocking collectives, turn(): squares = lax.psum(partial_sq, 'chan')  603 us
    ppermute x10, starting transfers between devices, shifted(): lax.ppermute(value, axis, [(source, source + steps) for source in range(i...  77.3 us
    dot_general x10, matrix products, add_rows(): return jnp.dot(shard_piece, weight, preferred_element_type=jnp.float32)  71.6 us
    gather x2, local copies, waits for them, and re-layouts, body(): modal.T[:, jnp.clip(inner_lag, 0, block_len - 1)]  46 us
    gather x2, local copies, waits for them, and re-layouts, body(): fir_section.T[:, jnp.clip(fir_lag, 0, fir_len - 1)]  46 us
    unnamed x16, local copies, waits for them, and re-layouts  34.9 us
  transfers between devices with their start and end apart: 20, of which 20 were waited for; matrix products, arithmetic and copies ran while one was open for 0% of the time, Pallas kernels for 0%

commit v1 on v0

--- a/solution.py
+++ b/solution.py
@@ -61,7 +61,11 @@
         rows_in = jnp.where(section_idx == 0, first_rows, incoming)
         inputs_f = rows_in.astype(jnp.float32)
         partial_sq = jnp.sum(inputs_f * inputs_f, axis=1)
-        squares = lax.psum(partial_sq, "chan")
+        squares = partial_sq
+        for hop in (1, 2, 4, 8, 16):
+            squares = squares + lax.ppermute(
+                squares, "chan", [(dev, dev ^ hop) for dev in range(32)]
+            )
         normed = (
             inputs_f * lax.rsqrt(squares[:, None] / width + EPSILON) * norm_gain.astype(jnp.float32)
         ).astype(jnp.bfloat16)

time: 1730 us -> 1260 us (0.73)
  blocking collectives: 603 us -> 0 us
  starting transfers between devices: 77.4 us -> 181 us
  waiting for transfers between devices: 783 us -> 811 us
    psum x10 -> x0, blocking collectives: 603 us -> none  [turn(): squares = lax.psum(partial_sq, 'chan')]
    ppermute x0 -> x50, starting transfers between devices: none -> 104 us  [turn(): lax.ppermute(squares, 'chan', [(dev, dev ^ hop) for dev in range(32)])]
    ppermute x0 -> x50, waiting for transfers between devices: none -> 82.1 us  [turn(): lax.ppermute(squares, 'chan', [(dev, dev ^ hop) for dev in range(32)])]
    all_gather x10, waiting for transfers between devices: 778 us -> 725 us  [turn(): projected = add_rows(lax.all_gather(normed, 'chan', axis=1, tiled=True))]
  transfers between devices with their start and end apart: 20 -> 70, of which waited for: 20 -> 70; matrix products, arithmetic and copies ran while one was open for 0% -> 0% of each run, Pallas kernels for 0% -> 0%
where the time goes in v1:
time: 1260 us
  waiting for transfers between devices  811 us (64%)
  starting transfers between devices  181 us (14%)
  local copies, waits for them, and re-layouts  136 us (11%)
  matrix products  88.7 us (7%)
  other arithmetic  21 us (2%)
  between operations  13.5 us (1%)
    all_gather x10, waiting for transfers between devices, turn(): projected = add_rows(lax.all_gather(normed, 'chan', axis=1, tiled=True))  725 us
    ppermute x50, starting transfers between devices, turn(): lax.ppermute(squares, 'chan', [(dev, dev ^ hop) for dev in range(32)])  104 us
    ppermute x50, waiting for transfers between devices, turn(): lax.ppermute(squares, 'chan', [(dev, dev ^ hop) for dev in range(32)])  82.1 us
    ppermute x10, starting transfers between devices, shifted(): lax.ppermute(value, axis, [(source, source + steps) for source in range(i...  77.3 us
    dot_general x10, matrix products, add_rows(): return jnp.dot(shard_piece, weight, preferred_element_type=jnp.float32)  71.6 us
    gather x2, local copies, waits for them, and re-layouts, body(): modal.T[:, jnp.clip(inner_lag, 0, block_len - 1)]  46 us
    gather x2, local copies, waits for them, and re-layouts, body(): fir_section.T[:, jnp.clip(fir_lag, 0, fir_len - 1)]  46 us
    unnamed x16, local copies, waits for them, and re-layouts  34.9 us
  transfers between devices with their start and end apart: 70, of which 70 were waited for; matrix products, arithmetic and copies ran while one was open for 0% of the time, Pallas kernels for 0%

profile of v1, /device:TPU:1, one launch (start us, length us, event | category | flops | bytes accessed | tf_op | source)
XLA Modules:
  0.0 1260.0 jit_solution(9477367265739533521)
XLA Ops:
  7.2 16.7 %copy.26 = bf16[1,8192,3,256]{1,3,2,0:T(8,128)(2,1)} copy(bf16[1,8192,3,256]{3,1,2,0:T(8,128)(2,1)} %param.11) | data formatting | bytes 25165824 | tf_op args[2]
  23.9 16.7 %copy.33 = bf16[8192,768]{1,0:T(8,128)(2,1)} copy(bf16[8192,768]{0,1:T(8,128)(2,1)} %bitcast.86) | data formatting | bytes 25165824
  41.1 41.1 %gather_fusion.1 = f32[12288,16]{1,0:T(8,128)} fusion(f32[16,64]{0,1:T(8,128)S(1)} %multiply_reduce_fusion, s32[12288]{0:T(1024)S(1)} %broadcast_clamp_fusion), kind=kCustom, calls=%fused_computation.1 | custom fusion | bytes 1622016 | tf_op jit(solution)/shard_map/gather | solution.py:43
  87.4 41.1 %gather_fusion = f32[12288,16]{1,0:T(8,128)} fusion(f32[16,128]{0,1:T(8,128)S(1)} %bitcast.82, s32[12288]{0:T(1024)S(1)} %broadcast_clamp_fusion.1), kind=kCustom, calls=%fused_computation | custom fusion | bytes 1622016 | tf_op jit(solution)/shard_map/gather | solution.py:37
  133.8 1118.7 %while.22 = (s32[]{:T(128)}, bf16[64,256]{1,0:T(8,128)(2,1)S(1)}, f32[2,3,256]{2,1,0:T(4,128)S(1)}, f32[128,256]{0,1:T(8,128)S(1)}, f32[16,16,16]{0,2,1:T(8,128)...) while((s32[]{:T(128)}, bf16[64,256]{1,0:T(8,128)(2,1)S(1)}, ...), condition=%wide.region_2.3_spmd.clone.clone.clone, body=%wide.region_0.2_spmd.clone.clone.clone.sunk | while | flops 850173568 | bytes 21383052 | solution.py:107
  157.5 74.3 %all-gather.2.cloned.1.call-done = bf16[64,8192]{1,0:T(8,128)(2,1)} async-done(((bf16[64,256]{1,0:T(8,128)(2,1)}), bf16[64,8192]{1,0:T(8,128)(2,1)}) %all-gather.2.cloned.1.call-update) | async-done | bytes 1048592 | tf_op jit(solution)/shard_map/while/body/eval_jaxpr/all_gather | solution.py:72
  270.9 72.3 %all-gather.2.cloned.1.call-done = bf16[64,8192]{1,0:T(8,128)(2,1)} async-done(((bf16[64,256]{1,0:T(8,128)(2,1)}), bf16[64,8192]{1,0:T(8,128)(2,1)}) %all-gather.2.cloned.1.call-update) | async-done | bytes 1048592 | tf_op jit(solution)/shard_map/while/body/eval_jaxpr/all_gather | solution.py:72
  352.3 7.7 collective-permute-start.5
  382.4 72.3 %all-gather.2.cloned.1.call-done = bf16[64,8192]{1,0:T(8,128)(2,1)} async-done(((bf16[64,256]{1,0:T(8,128)(2,1)}), bf16[64,8192]{1,0:T(8,128)(2,1)}) %all-gather.2.cloned.1.call-update) | async-done | bytes 1048592 | tf_op jit(solution)/shard_map/while/body/eval_jaxpr/all_gather | solution.py:72
  463.8 7.7 collective-permute-start.5
  493.8 72.3 %all-gather.2.cloned.1.call-done = bf16[64,8192]{1,0:T(8,128)(2,1)} async-done(((bf16[64,256]{1,0:T(8,128)(2,1)}), bf16[64,8192]{1,0:T(8,128)(2,1)}) %all-gather.2.cloned.1.call-update) | async-done | bytes 1048592 | tf_op jit(solution)/shard_map/while/body/eval_jaxpr/all_gather | solution.py:72
  575.2 7.7 collective-permute-start.5
  605.2 72.3 %all-gather.2.cloned.1.call-done = bf16[64,8192]{1,0:T(8,128)(2,1)} async-done(((bf16[64,256]{1,0:T(8,128)(2,1)}), bf16[64,8192]{1,0:T(8,128)(2,1)}) %all-gather.2.cloned.1.call-update) | async-done | bytes 1048592 | tf_op jit(solution)/shard_map/while/body/eval_jaxpr/all_gather | solution.py:72
  686.6 7.7 collective-permute-start.5
  716.7 72.3 %all-gather.2.cloned.1.call-done = bf16[64,8192]{1,0:T(8,128)(2,1)} async-done(((bf16[64,256]{1,0:T(8,128)(2,1)}), bf16[64,8192]{1,0:T(8,128)(2,1)}) %all-gather.2.cloned.1.call-update) | async-done | bytes 1048592 | tf_op jit(solution)/shard_map/while/body/eval_jaxpr/all_gather | solution.py:72
  798.1 7.7 collective-permute-start.5
  828.1 72.3 %all-gather.2.cloned.1.call-done = bf16[64,8192]{1,0:T(8,128)(2,1)} async-done(((bf16[64,256]{1,0:T(8,128)(2,1)}), bf16[64,8192]{1,0:T(8,128)(2,1)}) %all-gather.2.cloned.1.call-update) | async-done | bytes 1048592 | tf_op jit(solution)/shard_map/while/body/eval_jaxpr/all_gather | solution.py:72
  909.5 7.7 collective-permute-start.5
  939.5 72.3 %all-gather.2.cloned.1.call-done = bf16[64,8192]{1,0:T(8,128)(2,1)} async-done(((bf16[64,256]{1,0:T(8,128)(2,1)}), bf16[64,8192]{1,0:T(8,128)(2,1)}) %all-gather.2.cloned.1.call-update) | async-done | bytes 1048592 | tf_op jit(solution)/shard_map/while/body/eval_jaxpr/all_gather | solution.py:72
  1020.9 7.7 collective-permute-start.5
  1051.0 72.3 %all-gather.2.cloned.1.call-done = bf16[64,8192]{1,0:T(8,128)(2,1)} async-done(((bf16[64,256]{1,0:T(8,128)(2,1)}), bf16[64,8192]{1,0:T(8,128)(2,1)}) %all-gather.2.cloned.1.call-update) | async-done | bytes 1048592 | tf_op jit(solution)/shard_map/while/body/eval_jaxpr/all_gather | solution.py:72
  1132.4 7.7 collective-permute-start.5
  1162.4 72.3 %all-gather.2.cloned.1.call-done = bf16[64,8192]{1,0:T(8,128)(2,1)} async-done(((bf16[64,256]{1,0:T(8,128)(2,1)}), bf16[64,8192]{1,0:T(8,128)(2,1)}) %all-gather.2.cloned.1.call-update) | async-done | bytes 1048592 | tf_op jit(solution)/shard_map/while/body/eval_jaxpr/all_gather | solution.py:72
  1243.8 7.7 collective-permute-start.5
  (429 shorter events, 328.4 us)
Async XLA Ops:
  133.8 98.0 %all-gather.2.cloned.1.call-start = ((), (), s32[]{:S(2)}) async-start(), calls=%async_computation | async-start | bytes 1081344 | tf_op jit(solution)/shard_map/while/body/eval_jaxpr/all_gather | solution.py:72
  149.7 7.0 collective-permute-start.4
  240.9 8.7 collective-permute-start.5
  249.7 93.6 %all-gather.2.cloned.1.call-start = ((), (), s32[]{:S(2)}) async-start(), calls=%async_computation | async-start | bytes 1081344 | tf_op jit(solution)/shard_map/while/body/eval_jaxpr/all_gather | solution.py:72
  263.9 6.3 collective-permute-start.4
  352.3 8.7 collective-permute-start.5
  361.1 93.6 %all-gather.2.cloned.1.call-start = ((), (), s32[]{:S(2)}) async-start(), calls=%async_computation | async-start | bytes 1081344 | tf_op jit(solution)/shard_map/while/body/eval_jaxpr/all_gather | solution.py:72
  375.3 6.3 collective-permute-start.4
  463.8 8.7 collective-permute-start.5
  472.5 93.6 %all-gather.2.cloned.1.call-start = ((), (), s32[]{:S(2)}) async-start(), calls=%async_computation | async-start | bytes 1081344 | tf_op jit(solution)/shard_map/while/body/eval_jaxpr/all_gather | solution.py:72
  486.7 6.3 collective-permute-start.4
  575.2 8.7 collective-permute-start.5
  584.0 93.6 %all-gather.2.cloned.1.call-start = ((), (), s32[]{:S(2)}) async-start(), calls=%async_computation | async-start | bytes 1081344 | tf_op jit(solution)/shard_map/while/body/eval_jaxpr/all_gather | solution.py:72
  686.6 8.7 collective-permute-start.5
  695.4 93.6 %all-gather.2.cloned.1.call-start = ((), (), s32[]{:S(2)}) async-start(), calls=%async_computation | async-start | bytes 1081344 | tf_op jit(solution)/shard_map/while/body/eval_jaxpr/all_gather | solution.py:72
  798.1 8.7 collective-permute-start.5
  806.8 93.6 %all-gather.2.cloned.1.call-start = ((), (), s32[]{:S(2)}) async-start(), calls=%async_computation | async-start | bytes 1081344 | tf_op jit(solution)/shard_map/while/body/eval_jaxpr/all_gather | solution.py:72
  909.5 8.7 collective-permute-start.5
  918.2 93.6 %all-gather.2.cloned.1.call-start = ((), (), s32[]{:S(2)}) async-start(), calls=%async_computation | async-start | bytes 1081344 | tf_op jit(solution)/shard_map/while/body/eval_jaxpr/all_gather | solution.py:72
  1020.9 8.7 collective-permute-start.5
  1029.7 93.6 %all-gather.2.cloned.1.call-start = ((), (), s32[]{:S(2)}) async-start(), calls=%async_computation | async-start | bytes 1081344 | tf_op jit(solution)/shard_map/while/body/eval_jaxpr/all_gather | solution.py:72
  1132.4 8.7 collective-permute-start.5
  1141.1 93.6 %all-gather.2.cloned.1.call-start = ((), (), s32[]{:S(2)}) async-start(), calls=%async_computation | async-start | bytes 1081344 | tf_op jit(solution)/shard_map/while/body/eval_jaxpr/all_gather | solution.py:72
  1243.8 8.7 collective-permute-start.5
  (51 other events, 292.2 us)
Sparse Core Ops, SparseCore 0:
  157.6 74.1 all-gather.1
  271.0 72.1 all-gather.1
  382.4 72.1 all-gather.1
  493.9 72.1 all-gather.1
  605.3 72.1 all-gather.1
  716.7 72.1 all-gather.1
  828.2 72.1 all-gather.1
  939.6 72.1 all-gather.1
  1051.0 72.1 all-gather.1
  1162.5 72.1 all-gather.1
